TPU v7x, 128 devices: a whole 4x4x4 slice. The times are simulated.
128 devices in a mesh: row: 8 (over z, core), col: 16 (over x, y).
Axes of the slice: x: 4, y: 4, z: 4, core: 2. Of those that a mesh axis runs over, the one named last changes fastest.
Arguments:
- rate_terms: bfloat16 [6, 8192, 8192], P(None, 'row', 'col'), may hold values from -1 to 1
- populations: float32 [8192, 256], P(('row', 'col')), may hold values from 0.05 to 1
- temp_bins: int32 [256], replicated, may hold values from 0 to 63
- bin_coeffs: float32 [64, 6], replicated, may hold values from -1 to 1
Outputs:
- updated: float32 [8192, 256], P(('row', 'col'))
All inputs are finite; a program needn't handle non-finite values.
Results may differ from a plain program's by a relative error of at most 0.0011.
Values may be sent and summed in bfloat16 or wider, within the bound.
No kernel may reach another device: no remote copies, remote signals or barrier semaphores. Data moves between devices by JAX's collectives and lax.ppermute only.
A program may use at most 64 MiB of HBM per device.

v0:
```python
import math
import jax
import jax.numpy as jnp
from jax import lax
from jax.sharding import PartitionSpec as P

KRYLOV = 4
TAYLOR = 8
epsilon = 1e-06
step_size = 1.0


def body(rate_terms, populations, temp_bins, bin_coeffs):
    col_id = lax.axis_index("col")
    n_terms = rate_terms.shape[0]
    row_rows = rate_terms.shape[1]
    col_rows = rate_terms.shape[2]
    n_bins = bin_coeffs.shape[0]
    n_cells = populations.shape[1]
    onehot = (temp_bins[:, None] == jnp.arange(n_bins, dtype=jnp.int32)[None, :]).astype(
        jnp.float32
    )
    weights = jnp.dot(onehot, bin_coeffs, precision=lax.Precision.HIGHEST)
    weights_t = weights.T
    stacked = rate_terms.reshape(n_terms * row_rows, col_rows)

    def apply_rates(vector):
        rounded = vector.astype(jnp.bfloat16)
        gathered = lax.all_gather(rounded, ("row", "col"), axis=0, tiled=True)
        operand = lax.dynamic_slice_in_dim(gathered, col_id * col_rows, col_rows, 0)
        products = jnp.dot(stacked, operand, preferred_element_type=jnp.float32).reshape(
            n_terms, row_rows, n_cells
        )
        partial_value = jnp.sum(products * weights_t[:, None, :], axis=0)
        return lax.psum_scatter(partial_value, "col", scatter_dimension=0, tiled=True)

    def norm_of(vector):
        squares = lax.psum(jnp.sum(vector * vector, axis=0), ("row", "col"))
        return jnp.sqrt(squares + epsilon)

    force = apply_rates(populations)
    scale_norm = norm_of(force)
    basis = [force / scale_norm[None, :]]
    zero_row = jnp.zeros((n_cells,), jnp.float32)
    hessen = [[zero_row for j in range(KRYLOV)] for i in range(KRYLOV)]
    for j in range(KRYLOV):
        fresh = apply_rates(basis[j])
        for i in range(j + 1):
            correlation = lax.psum(jnp.sum(basis[i] * fresh, axis=0), ("row", "col"))
            fresh = fresh - correlation[None, :] * basis[i]
            hessen[i][j] = correlation
        if j < KRYLOV - 1:
            length = norm_of(fresh)
            hessen[j + 1][j] = length
            basis.append(fresh / length[None, :])
    hmat = jnp.stack([jnp.stack(line) for line in hessen]) * step_size
    first_unit = jnp.zeros((KRYLOV, n_cells), jnp.float32).at[0].set(1.0)
    coeffs = first_unit / float(math.factorial(TAYLOR + 1))
    for k in range(TAYLOR - 1, -1, -1):
        coeffs = jnp.sum(hmat * coeffs[None, :, :], axis=1) + first_unit / float(
            math.factorial(k + 1)
        )
    update = jnp.zeros(populations.shape, jnp.float32)
    for i in range(KRYLOV):
        update = update + coeffs[i][None, :] * basis[i]
    return populations + step_size * scale_norm[None, :] * update


def solution(mesh):
    placed = (P(None, "row", "col"), P(("row", "col"), None), P(), P())
    return jax.shard_map(
        body, mesh=mesh, in_specs=placed, out_specs=P(("row", "col"), None), check_vma=False
    )
```

profile of v0, /device:TPU:1, one launch (start us, length us, event | category | flops | bytes accessed | tf_op | source)
XLA Modules:
  0.0 1696.6 jit_solution(16298154041316169169)
XLA Ops:
  6.5 1.5 convert_element_type.16
  8.0 0.0 reduce-scatter.6.cloned.1.call-start
  8.1 0.9 convolution_bitcast_fusion.5
  9.0 71.7 %all-gather.6.cloned.1.call-done = bf16[8192,256]{1,0:T(8,128)(2,1)} async-done(((bf16[64,256]{1,0:T(8,128)(2,1)}), bf16[8192,256]{1,0:T(8,128)(2,1)}) %all-gather.6.cloned.1.call-update) | async-done | bytes 4194320 | tf_op jit(solution)/shard_map/all_gather | solution.py:29
  80.6 7.4 convolution_bitcast_fusion.4
  88.0 6.5 copy.11
  94.6 4.4 multiply_reduce_fusion.4
  99.0 69.5 %reduce-scatter.6.cloned.1.call-done = f32[64,256]{1,0:T(8,128)} async-done(((f32[1024,256]{1,0:T(8,128)}), f32[64,256]{1,0:T(8,128)}) %reduce-scatter.6.cloned.1.call-update) | async-done | bytes 65552 | tf_op jit(solution)/shard_map/reduce_scatter | solution.py:35
  168.5 0.9 multiply_reduce_fusion.18
  169.4 66.1 %psum.98 = f32[256]{0:T(256)S(1)} all-reduce(f32[256]{0:T(256)S(1)} %multiply_reduce_fusion.18), channel_id=1, replica_groups=mesh['row'=8,'col'=16] {'row','col'}, use_global_device_ids=true, to_apply=%region_3.0 | all-reduce | flops 256 | bytes 2048 | tf_op jit(solution)/shard_map/psum | solution.py:38
  235.5 1.5 fusion.13
  237.1 63.4 %all-gather.8.cloned.1.call-done = bf16[8192,256]{1,0:T(8,128)(2,1)} async-done(((bf16[64,256]{1,0:T(8,128)(2,1)}), bf16[8192,256]{1,0:T(8,128)(2,1)}) %all-gather.8.cloned.1.call-update) | async-done | bytes 4194320 | tf_op jit(solution)/shard_map/all_gather | solution.py:29
  300.5 7.4 convolution_bitcast_fusion.3
  307.9 6.5 copy.12
  314.4 4.4 multiply_reduce_fusion.3
  318.8 0.0 all-gather.10.cloned.1.call-start
  318.9 69.5 %reduce-scatter.8.cloned.1.call-done = f32[64,256]{1,0:T(8,128)} async-done(((f32[1024,256]{1,0:T(8,128)}), f32[64,256]{1,0:T(8,128)}) %reduce-scatter.8.cloned.1.call-update) | async-done | bytes 65552 | tf_op jit(solution)/shard_map/reduce_scatter | solution.py:35
  388.4 0.9 multiply_reduce_fusion.17
  389.3 66.1 %psum.99 = f32[256]{0:T(256)S(1)} all-reduce(f32[256]{0:T(256)S(1)} %multiply_reduce_fusion.17), channel_id=1, replica_groups=mesh['row'=8,'col'=16] {'row','col'}, use_global_device_ids=true, to_apply=%region_7.0 | all-reduce | flops 256 | bytes 2048 | tf_op jit(solution)/shard_map/psum | solution.py:49
  455.4 0.9 multiply_reduce_fusion.16
  456.3 62.5 %psum.100 = f32[256]{0:T(256)S(1)} all-reduce(f32[256]{0:T(256)S(1)} %multiply_reduce_fusion.16), channel_id=1, replica_groups=mesh['row'=8,'col'=16] {'row','col'}, use_global_device_ids=true, to_apply=%region_9.0 | all-reduce | flops 256 | bytes 2048 | tf_op jit(solution)/shard_map/psum | solution.py:38
  518.8 1.5 fusion.14
  520.3 0.2 reduce-scatter.10.cloned.1.call-start
  520.5 63.9 %all-gather.10.cloned.1.call-done = bf16[8192,256]{1,0:T(8,128)(2,1)} async-done(((bf16[64,256]{1,0:T(8,128)(2,1)}), bf16[8192,256]{1,0:T(8,128)(2,1)}) %all-gather.10.cloned.1.call-update) | async-done | bytes 4194320 | tf_op jit(solution)/shard_map/all_gather | solution.py:29
  584.4 7.4 convolution_bitcast_fusion.2
  591.8 6.5 copy.13
  598.4 4.4 multiply_reduce_fusion.2
  602.8 69.5 %reduce-scatter.10.cloned.1.call-done = f32[64,256]{1,0:T(8,128)} async-done(((f32[1024,256]{1,0:T(8,128)}), f32[64,256]{1,0:T(8,128)}) %reduce-scatter.10.cloned.1.call-update) | async-done | bytes 65552 | tf_op jit(solution)/shard_map/reduce_scatter | solution.py:35
  672.3 0.9 multiply_reduce_fusion.15
  673.2 66.1 %psum.101 = f32[256]{0:T(256)S(1)} all-reduce(f32[256]{0:T(256)S(1)} %multiply_reduce_fusion.15), channel_id=1, replica_groups=mesh['row'=8,'col'=16] {'row','col'}, use_global_device_ids=true, to_apply=%region_13.0 | all-reduce | flops 256 | bytes 2048 | tf_op jit(solution)/shard_map/psum | solution.py:49
  739.3 0.9 multiply_reduce_fusion.14
  740.2 62.5 %psum.102 = f32[256]{0:T(256)S(1)} all-reduce(f32[256]{0:T(256)S(1)} %multiply_reduce_fusion.14), channel_id=1, replica_groups=mesh['row'=8,'col'=16] {'row','col'}, use_global_device_ids=true, to_apply=%region_15.0 | all-reduce | flops 256 | bytes 2048 | tf_op jit(solution)/shard_map/psum | solution.py:49
  802.7 0.9 multiply_reduce_fusion.13
  803.6 64.0 %psum.103 = f32[256]{0:T(256)S(1)} all-reduce(f32[256]{0:T(256)S(1)} %get-tuple-element.21), channel_id=1, replica_groups=mesh['row'=8,'col'=16] {'row','col'}, use_global_device_ids=true, to_apply=%region_17.0 | all-reduce | flops 256 | bytes 2048 | tf_op jit(solution)/shard_map/psum | solution.py:38
  867.6 0.6 fusion.12
  868.3 0.0 reduce-scatter.12.cloned.1.call-start
  868.3 63.5 %all-gather.12.cloned.1.call-done = bf16[8192,256]{1,0:T(8,128)(2,1)} async-done(((bf16[64,256]{1,0:T(8,128)(2,1)}), bf16[8192,256]{1,0:T(8,128)(2,1)}) %all-gather.12.cloned.1.call-update) | async-done | bytes 4194320 | tf_op jit(solution)/shard_map/all_gather | solution.py:29
  931.8 7.4 convolution_bitcast_fusion.1
  939.2 6.5 copy.14
  945.7 4.4 multiply_reduce_fusion.1
  950.2 69.5 %reduce-scatter.12.cloned.1.call-done = f32[64,256]{1,0:T(8,128)} async-done(((f32[1024,256]{1,0:T(8,128)}), f32[64,256]{1,0:T(8,128)}) %reduce-scatter.12.cloned.1.call-update) | async-done | bytes 65552 | tf_op jit(solution)/shard_map/reduce_scatter | solution.py:35
  1019.7 0.9 multiply_reduce_fusion.12
  1020.6 66.1 %psum.104 = f32[256]{0:T(256)S(1)} all-reduce(f32[256]{0:T(256)S(1)} %multiply_reduce_fusion.12), channel_id=1, replica_groups=mesh['row'=8,'col'=16] {'row','col'}, use_global_device_ids=true, to_apply=%region_21.0 | all-reduce | flops 256 | bytes 2048 | tf_op jit(solution)/shard_map/psum | solution.py:49
  1086.7 0.9 multiply_reduce_fusion.11
  1087.6 62.5 %psum.105 = f32[256]{0:T(256)S(1)} all-reduce(f32[256]{0:T(256)S(1)} %multiply_reduce_fusion.11), channel_id=1, replica_groups=mesh['row'=8,'col'=16] {'row','col'}, use_global_device_ids=true, to_apply=%region_23.0 | all-reduce | flops 256 | bytes 2048 | tf_op jit(solution)/shard_map/psum | solution.py:49
  1150.1 0.9 multiply_reduce_fusion.10
  1151.0 64.3 %psum.106 = f32[256]{0:T(256)S(1)} all-reduce(f32[256]{0:T(256)S(1)} %get-tuple-element.19), channel_id=1, replica_groups=mesh['row'=8,'col'=16] {'row','col'}, use_global_device_ids=true, to_apply=%region_25.0 | all-reduce | flops 256 | bytes 2048 | tf_op jit(solution)/shard_map/psum | solution.py:49
  1215.2 62.5 %psum.107 = f32[256]{0:T(256)S(1)} all-reduce(f32[256]{0:T(256)S(1)} %multiply_reduce_fusion.9), channel_id=1, replica_groups=mesh['row'=8,'col'=16] {'row','col'}, use_global_device_ids=true, to_apply=%region_27.0 | all-reduce | flops 256 | bytes 2048 | tf_op jit(solution)/shard_map/psum | solution.py:38
  1277.8 0.6 fusion.6
  1278.5 64.1 %all-gather.14.cloned.1.call-done = bf16[8192,256]{1,0:T(8,128)(2,1)} async-done(((bf16[64,256]{1,0:T(8,128)(2,1)}), bf16[8192,256]{1,0:T(8,128)(2,1)}) %all-gather.14.cloned.1.call-update) | async-done | bytes 4194320 | tf_op jit(solution)/shard_map/all_gather | solution.py:29
  1342.6 7.4 convolution_bitcast_fusion
  1350.0 6.5 copy.15
  1356.7 4.4 multiply_reduce_fusion
  1361.1 69.5 %reduce-scatter.14.cloned.1.call-done = f32[64,256]{1,0:T(8,128)} async-done(((f32[1024,256]{1,0:T(8,128)}), f32[64,256]{1,0:T(8,128)}) %reduce-scatter.14.cloned.1.call-update) | async-done | bytes 65552 | tf_op jit(solution)/shard_map/reduce_scatter | solution.py:35
  1430.6 0.9 multiply_reduce_fusion.8
  1431.5 66.1 %psum.108 = f32[256]{0:T(256)S(1)} all-reduce(f32[256]{0:T(256)S(1)} %multiply_reduce_fusion.8), channel_id=1, replica_groups=mesh['row'=8,'col'=16] {'row','col'}, use_global_device_ids=true, to_apply=%region_31.0 | all-reduce | flops 256 | bytes 2048 | tf_op jit(solution)/shard_map/psum | solution.py:49
  1497.7 0.9 multiply_reduce_fusion.7
  1498.5 62.5 %psum.109 = f32[256]{0:T(256)S(1)} all-reduce(f32[256]{0:T(256)S(1)} %multiply_reduce_fusion.7), channel_id=1, replica_groups=mesh['row'=8,'col'=16] {'row','col'}, use_global_device_ids=true, to_apply=%region_33.0 | all-reduce | flops 256 | bytes 2048 | tf_op jit(solution)/shard_map/psum | solution.py:49
  1561.0 0.9 multiply_reduce_fusion.6
  1561.9 64.0 %psum.110 = f32[256]{0:T(256)S(1)} all-reduce(f32[256]{0:T(256)S(1)} %get-tuple-element.17), channel_id=1, replica_groups=mesh['row'=8,'col'=16] {'row','col'}, use_global_device_ids=true, to_apply=%region_35.0 | all-reduce | flops 256 | bytes 2048 | tf_op jit(solution)/shard_map/psum | solution.py:49
  1626.0 62.5 %psum.111 = f32[1,256]{1,0:T(1,128)S(1)} all-reduce(f32[1,256]{1,0:T(1,128)S(1)} %bitcast.72), channel_id=1, replica_groups=mesh['row'=8,'col'=16] {'row','col'}, use_global_device_ids=true, to_apply=%region_37.0 | all-reduce | flops 256 | bytes 2048 | tf_op jit(solution)/shard_map/psum | solution.py:49
  1688.5 0.1 maximum_bitcast_fusion.3
  1688.6 0.1 maximum_bitcast_fusion.2
  1689.1 0.7 multiply_add_fusion
  (69 shorter events, 0.8 us)
Async XLA Ops:
  6.5 1.6 copy-start
  6.5 74.1 %all-gather.6.cloned.1.call-start = ((), (), s32[]{:S(2)}) async-start(), calls=%async_computation.5 | async-start | bytes 4227072 | tf_op jit(solution)/shard_map/all_gather | solution.py:29
  8.0 160.5 %reduce-scatter.6.cloned.1.call-start = ((), (), s32[]{:S(2)}) async-start(), calls=%async_computation.6 | async-start | bytes 1114112 | tf_op jit(solution)/shard_map/reduce_scatter | solution.py:35
  98.9 201.5 %all-gather.8.cloned.1.call-start = ((), (), s32[]{:S(2)}) async-start(), calls=%async_computation.7 | async-start | bytes 4227072 | tf_op jit(solution)/shard_map/all_gather | solution.py:29
  237.0 151.4 %reduce-scatter.8.cloned.1.call-start = ((), (), s32[]{:S(2)}) async-start(), calls=%async_computation.8 | async-start | bytes 1114112 | tf_op jit(solution)/shard_map/reduce_scatter | solution.py:35
  314.4 74.0 %copy-start.2 = (f32[64,256]{1,0:T(8,128)S(1)}, f32[64,256]{1,0:T(8,128)}, u32[]{:S(2)}) copy-start(f32[64,256]{1,0:T(8,128)} %reduce-scatter.6.cloned.1.call-done) | copy-start | bytes 196612
  318.8 265.6 %all-gather.10.cloned.1.call-start = ((), (), s32[]{:S(2)}) async-start(), calls=%async_computation.9 | async-start | bytes 4227072 | tf_op jit(solution)/shard_map/all_gather | solution.py:29
  520.3 152.1 %reduce-scatter.10.cloned.1.call-start = ((), (), s32[]{:S(2)}) async-start(), calls=%async_computation.10 | async-start | bytes 1114112 | tf_op jit(solution)/shard_map/reduce_scatter | solution.py:35
  598.4 141.0 %copy-start.3 = (f32[64,256]{1,0:T(8,128)S(1)}, f32[64,256]{1,0:T(8,128)}, u32[]{:S(2)}) copy-start(f32[64,256]{1,0:T(8,128)} %reduce-scatter.8.cloned.1.call-done) | copy-start | bytes 196612
  602.7 329.1 %all-gather.12.cloned.1.call-start = ((), (), s32[]{:S(2)}) async-start(), calls=%async_computation.11 | async-start | bytes 4227072 | tf_op jit(solution)/shard_map/all_gather | solution.py:29
  868.3 151.4 %reduce-scatter.12.cloned.1.call-start = ((), (), s32[]{:S(2)}) async-start(), calls=%async_computation.12 | async-start | bytes 1114112 | tf_op jit(solution)/shard_map/reduce_scatter | solution.py:35
  950.1 392.5 %all-gather.14.cloned.1.call-start = ((), (), s32[]{:S(2)}) async-start(), calls=%async_computation.13 | async-start | bytes 4227072 | tf_op jit(solution)/shard_map/all_gather | solution.py:29
  1278.5 152.2 %reduce-scatter.14.cloned.1.call-start = ((), (), s32[]{:S(2)}) async-start(), calls=%async_computation.14 | async-start | bytes 1114112 | tf_op jit(solution)/shard_map/reduce_scatter | solution.py:35
  1350.0 339.7 %copy-start.1 = (f32[64,6]{0,1:T(8,128)S(1)}, f32[64,6]{0,1:T(8,128)}, u32[]{:S(2)}) copy-start(f32[64,6]{0,1:T(8,128)} %param.9) | copy-start | bytes 4612
  1356.6 332.1 %copy-start.12 = (f32[4,256]{1,0:T(4,128)S(1)}, f32[4,256]{1,0:T(4,128)}, u32[]{:S(2)}) copy-start(f32[4,256]{1,0:T(4,128)} %constant.71.clone.1) | copy-start | bytes 12292
  1356.6 332.1 %copy-start.11 = (f32[4,256]{1,0:T(4,128)S(1)}, f32[4,256]{1,0:T(4,128)}, u32[]{:S(2)}) copy-start(f32[4,256]{1,0:T(4,128)} %constant.72.clone.1) | copy-start | bytes 12292
  1356.6 332.2 %copy-start.10 = (f32[4,256]{1,0:T(4,128)S(1)}, f32[4,256]{1,0:T(4,128)}, u32[]{:S(2)}) copy-start(f32[4,256]{1,0:T(4,128)} %constant.73.clone.1) | copy-start | bytes 12292
  1356.6 332.2 %copy-start.9 = (f32[4,256]{1,0:T(4,128)S(1)}, f32[4,256]{1,0:T(4,128)}, u32[]{:S(2)}) copy-start(f32[4,256]{1,0:T(4,128)} %constant.74.clone.1) | copy-start | bytes 12292
  1356.6 332.3 %copy-start.8 = (f32[4,256]{1,0:T(4,128)S(1)}, f32[4,256]{1,0:T(4,128)}, u32[]{:S(2)}) copy-start(f32[4,256]{1,0:T(4,128)} %constant.75.clone.1) | copy-start | bytes 12292
  1356.6 332.3 %copy-start.7 = (f32[4,256]{1,0:T(4,128)S(1)}, f32[4,256]{1,0:T(4,128)}, u32[]{:S(2)}) copy-start(f32[4,256]{1,0:T(4,128)} %constant.76.clone.1) | copy-start | bytes 12292
  1356.6 332.3 %copy-start.6 = (f32[4,256]{1,0:T(4,128)S(1)}, f32[4,256]{1,0:T(4,128)}, u32[]{:S(2)}) copy-start(f32[4,256]{1,0:T(4,128)} %constant.77.clone.1) | copy-start | bytes 12292
  1356.6 332.4 %copy-start.5 = (f32[4,256]{1,0:T(4,128)S(1)}, f32[4,256]{1,0:T(4,128)}, u32[]{:S(2)}) copy-start(f32[4,256]{1,0:T(4,128)} %constant.78.clone.1) | copy-start | bytes 12292
  1356.6 332.4 %copy-start.4 = (f32[64,256]{1,0:T(8,128)S(1)}, f32[64,256]{1,0:T(8,128)}, u32[]{:S(2)}) copy-start(f32[64,256]{1,0:T(8,128)} %param.7) | copy-start | bytes 196612
Sparse Core Ops, SparseCore 0:
  10.5 70.1 all-gather.5
  99.1 69.4 reduce-scatter.5
  237.1 63.3 all-gather.7
  318.9 69.4 reduce-scatter.7
  520.4 64.0 all-gather.9
  602.9 69.4 reduce-scatter.9
  868.4 63.3 all-gather.11
  950.3 69.4 reduce-scatter.11
  1278.6 64.0 all-gather.13
  1361.2 69.3 reduce-scatter.13
where the time goes:
time: 1700 us
  blocking collectives  898 us (53%)
  waiting for transfers between devices  674 us (40%)
  other arithmetic  39.3 us (2%)
  matrix products  37.9 us (2%)
  local copies, waits for them, and re-layouts  32.7 us (2%)
    psum x10, blocking collectives, body(): correlation = lax.psum(jnp.sum(basis[i] * fresh, axis=0), ('row', 'col'))  643 us
    reduce_scatter x5, waiting for transfers between devices, apply_rates(): lax.psum_scatter(partial_value, 'col', scatter_dimension=0, tiled=True)  348 us
    all_gather x5, waiting for transfers between devices, apply_rates(): gathered = lax.all_gather(rounded, ('row', 'col'), axis=0, tiled=True)  327 us
    psum x4, blocking collectives, norm_of(): squares = lax.psum(jnp.sum(vector * vector, axis=0), ('row', 'col'))  255 us
    dot_general x5, matrix products, apply_rates(): jnp.dot(stacked, operand, preferred_element_type=jnp.float32)  37 us
  transfers between devices with their start and end apart: 10, of which 10 were waited for; matrix products, arithmetic and copies ran while one was open for 0% of the time, Pallas kernels for 0%

commit v1 on v0

--- a/solution.py
+++ b/solution.py
@@ -46,7 +46,8 @@
     for j in range(KRYLOV):
         fresh = apply_rates(basis[j])
         for i in range(j + 1):
-            correlation = lax.psum(jnp.sum(basis[i] * fresh, axis=0), ("row", "col"))
+            view = jnp.sum(basis[i] * fresh, axis=0)
+            correlation = jax.lax.psum(jax.lax.psum(view, "col"), "row")
             fresh = fresh - correlation[None, :] * basis[i]
             hessen[i][j] = correlation
         if j < KRYLOV - 1:

time: 1700 us -> 1550 us (0.912)
  blocking collectives: 898 us -> 754 us
    psum x10 -> x20, blocking collectives: 643 us -> 500 us  [body(): correlation = jax.lax.psum(jax.lax.psum(view, 'col'), 'row')]
where the time goes in v1:
time: 1550 us
  blocking collectives  754 us (49%)
  waiting for transfers between devices  675 us (44%)
  other arithmetic  39.3 us (3%)
  matrix products  37.9 us (2%)
  local copies, waits for them, and re-layouts  32.7 us (2%)
    psum x20, blocking collectives, body(): correlation = jax.lax.psum(jax.lax.psum(view, 'col'), 'row')  500 us
    reduce_scatter x5, waiting for transfers between devices, apply_rates(): lax.psum_scatter(partial_value, 'col', scatter_dimension=0, tiled=True)  348 us
    all_gather x5, waiting for transfers between devices, apply_rates(): gathered = lax.all_gather(rounded, ('row', 'col'), axis=0, tiled=True)  327 us
    psum x4, blocking collectives, norm_of(): squares = lax.psum(jnp.sum(vector * vector, axis=0), ('row', 'col'))  253 us
    dot_general x5, matrix products, apply_rates(): jnp.dot(stacked, operand, preferred_element_type=jnp.float32)  37 us
    dot_general x5, local copies, waits for them, and re-layouts, apply_rates(): jnp.dot(stacked, operand, preferred_element_type=jnp.float32)  32.6 us
  transfers between devices with their start and end apart: 10, of which 10 were waited for; matrix products, arithmetic and copies ran while one was open for 0% of the time, Pallas kernels for 0%

profile of v1, /device:TPU:1, one launch (start us, length us, event | category | flops | bytes accessed | tf_op | source)
XLA Modules:
  0.0 1552.7 jit_solution(1463091828336133136)
XLA Ops:
  6.5 1.5 convert_element_type.16
  8.1 0.9 convolution_bitcast_fusion.5
  9.0 71.7 %all-gather.6.cloned.1.call-done = bf16[8192,256]{1,0:T(8,128)(2,1)} async-done(((bf16[64,256]{1,0:T(8,128)(2,1)}), bf16[8192,256]{1,0:T(8,128)(2,1)}) %all-gather.6.cloned.1.call-update) | async-done | bytes 4194320 | tf_op jit(solution)/shard_map/all_gather | solution.py:29
  80.6 7.4 convolution_bitcast_fusion.4
  88.0 6.5 copy.11
  94.6 4.4 multiply_reduce_fusion.4
  99.0 69.5 %reduce-scatter.6.cloned.1.call-done = f32[64,256]{1,0:T(8,128)} async-done(((f32[1024,256]{1,0:T(8,128)}), f32[64,256]{1,0:T(8,128)}) %reduce-scatter.6.cloned.1.call-update) | async-done | bytes 65552 | tf_op jit(solution)/shard_map/reduce_scatter | solution.py:35
  169.4 66.1 %psum.168 = f32[256]{0:T(256)S(1)} all-reduce(f32[256]{0:T(256)S(1)} %multiply_reduce_fusion.18), channel_id=1, replica_groups=mesh['row'=8,'col'=16] {'row','col'}, use_global_device_ids=true, to_apply=%region_3.0 | all-reduce | flops 256 | bytes 2048 | tf_op jit(solution)/shard_map/psum | solution.py:38
  235.5 1.5 fusion.13
  237.1 63.4 %all-gather.8.cloned.1.call-done = bf16[8192,256]{1,0:T(8,128)(2,1)} async-done(((bf16[64,256]{1,0:T(8,128)(2,1)}), bf16[8192,256]{1,0:T(8,128)(2,1)}) %all-gather.8.cloned.1.call-update) | async-done | bytes 4194320 | tf_op jit(solution)/shard_map/all_gather | solution.py:29
  300.5 7.4 convolution_bitcast_fusion.3
  307.9 6.5 copy.12
  314.4 4.4 multiply_reduce_fusion.3
  318.9 69.5 %reduce-scatter.8.cloned.1.call-done = f32[64,256]{1,0:T(8,128)} async-done(((f32[1024,256]{1,0:T(8,128)}), f32[64,256]{1,0:T(8,128)}) %reduce-scatter.8.cloned.1.call-update) | async-done | bytes 65552 | tf_op jit(solution)/shard_map/reduce_scatter | solution.py:35
  388.4 0.9 multiply_reduce_fusion.17
  389.3 30.9 %psum.169 = f32[256]{0:T(256)S(1)} all-reduce(f32[256]{0:T(256)S(1)} %multiply_reduce_fusion.17), channel_id=1, replica_groups=mesh['row'=8,'col'=16] {'col'}, use_global_device_ids=true, to_apply=%region_7.0 | all-reduce | flops 256 | bytes 2048 | tf_op jit(solution)/shard_map/psum | solution.py:50
  420.2 21.4 %psum.170 = f32[256]{0:T(256)S(1)} all-reduce(f32[256]{0:T(256)S(1)} %psum.169), channel_id=1, replica_groups=mesh['row'=8,'col'=16] {'row'}, use_global_device_ids=true, to_apply=%region_8.0 | all-reduce | flops 256 | bytes 2048 | tf_op jit(solution)/shard_map/psum | solution.py:50
  441.6 0.9 multiply_reduce_fusion.16
  442.5 61.9 %psum.171 = f32[256]{0:T(256)S(1)} all-reduce(f32[256]{0:T(256)S(1)} %multiply_reduce_fusion.16), channel_id=1, replica_groups=mesh['row'=8,'col'=16] {'row','col'}, use_global_device_ids=true, to_apply=%region_10.0 | all-reduce | flops 256 | bytes 2048 | tf_op jit(solution)/shard_map/psum | solution.py:38
  504.4 1.5 fusion.14
  506.0 64.0 %all-gather.10.cloned.1.call-done = bf16[8192,256]{1,0:T(8,128)(2,1)} async-done(((bf16[64,256]{1,0:T(8,128)(2,1)}), bf16[8192,256]{1,0:T(8,128)(2,1)}) %all-gather.10.cloned.1.call-update) | async-done | bytes 4194320 | tf_op jit(solution)/shard_map/all_gather | solution.py:29
  570.0 7.4 convolution_bitcast_fusion.2
  577.4 6.5 copy.13
  583.9 4.4 multiply_reduce_fusion.2
  588.4 69.5 %reduce-scatter.10.cloned.1.call-done = f32[64,256]{1,0:T(8,128)} async-done(((f32[1024,256]{1,0:T(8,128)}), f32[64,256]{1,0:T(8,128)}) %reduce-scatter.10.cloned.1.call-update) | async-done | bytes 65552 | tf_op jit(solution)/shard_map/reduce_scatter | solution.py:35
  657.9 0.9 multiply_reduce_fusion.15
  658.7 31.1 %psum.172 = f32[256]{0:T(256)S(1)} all-reduce(f32[256]{0:T(256)S(1)} %multiply_reduce_fusion.15), channel_id=1, replica_groups=mesh['row'=8,'col'=16] {'col'}, use_global_device_ids=true, to_apply=%region_14.0 | all-reduce | flops 256 | bytes 2048 | tf_op jit(solution)/shard_map/psum | solution.py:50
  689.8 21.5 %psum.173 = f32[256]{0:T(256)S(1)} all-reduce(f32[256]{0:T(256)S(1)} %psum.172), channel_id=1, replica_groups=mesh['row'=8,'col'=16] {'row'}, use_global_device_ids=true, to_apply=%region_15.0 | all-reduce | flops 256 | bytes 2048 | tf_op jit(solution)/shard_map/psum | solution.py:50
  711.3 0.9 multiply_reduce_fusion.14
  712.2 28.8 %psum.174 = f32[256]{0:T(256)S(1)} all-reduce(f32[256]{0:T(256)S(1)} %multiply_reduce_fusion.14), channel_id=1, replica_groups=mesh['row'=8,'col'=16] {'col'}, use_global_device_ids=true, to_apply=%region_17.0 | all-reduce | flops 256 | bytes 2048 | tf_op jit(solution)/shard_map/psum | solution.py:50
  741.0 18.9 %psum.175 = f32[256]{0:T(256)S(1)} all-reduce(f32[256]{0:T(256)S(1)} %psum.174), channel_id=1, replica_groups=mesh['row'=8,'col'=16] {'row'}, use_global_device_ids=true, to_apply=%region_18.0 | all-reduce | flops 256 | bytes 2048 | tf_op jit(solution)/shard_map/psum | solution.py:50
  759.9 0.9 multiply_reduce_fusion.13
  760.8 63.2 %psum.176 = f32[256]{0:T(256)S(1)} all-reduce(f32[256]{0:T(256)S(1)} %get-tuple-element.21), channel_id=1, replica_groups=mesh['row'=8,'col'=16] {'row','col'}, use_global_device_ids=true, to_apply=%region_20.0 | all-reduce | flops 256 | bytes 2048 | tf_op jit(solution)/shard_map/psum | solution.py:38
  824.7 64.0 %all-gather.12.cloned.1.call-done = bf16[8192,256]{1,0:T(8,128)(2,1)} async-done(((bf16[64,256]{1,0:T(8,128)(2,1)}), bf16[8192,256]{1,0:T(8,128)(2,1)}) %all-gather.12.cloned.1.call-update) | async-done | bytes 4194320 | tf_op jit(solution)/shard_map/all_gather | solution.py:29
  888.7 7.4 convolution_bitcast_fusion.1
  896.1 6.5 copy.14
  902.6 4.4 multiply_reduce_fusion.1
  907.1 69.5 %reduce-scatter.12.cloned.1.call-done = f32[64,256]{1,0:T(8,128)} async-done(((f32[1024,256]{1,0:T(8,128)}), f32[64,256]{1,0:T(8,128)}) %reduce-scatter.12.cloned.1.call-update) | async-done | bytes 65552 | tf_op jit(solution)/shard_map/reduce_scatter | solution.py:35
  976.6 0.9 multiply_reduce_fusion.12
  977.5 30.9 %psum.177 = f32[256]{0:T(256)S(1)} all-reduce(f32[256]{0:T(256)S(1)} %multiply_reduce_fusion.12), channel_id=1, replica_groups=mesh['row'=8,'col'=16] {'col'}, use_global_device_ids=true, to_apply=%region_24.0 | all-reduce | flops 256 | bytes 2048 | tf_op jit(solution)/shard_map/psum | solution.py:50
  1008.4 21.4 %psum.178 = f32[256]{0:T(256)S(1)} all-reduce(f32[256]{0:T(256)S(1)} %psum.177), channel_id=1, replica_groups=mesh['row'=8,'col'=16] {'row'}, use_global_device_ids=true, to_apply=%region_25.0 | all-reduce | flops 256 | bytes 2048 | tf_op jit(solution)/shard_map/psum | solution.py:50
  1029.8 0.9 multiply_reduce_fusion.11
  1030.7 28.8 %psum.179 = f32[256]{0:T(256)S(1)} all-reduce(f32[256]{0:T(256)S(1)} %multiply_reduce_fusion.11), channel_id=1, replica_groups=mesh['row'=8,'col'=16] {'col'}, use_global_device_ids=true, to_apply=%region_27.0 | all-reduce | flops 256 | bytes 2048 | tf_op jit(solution)/shard_map/psum | solution.py:50
  1059.5 18.9 %psum.180 = f32[256]{0:T(256)S(1)} all-reduce(f32[256]{0:T(256)S(1)} %psum.179), channel_id=1, replica_groups=mesh['row'=8,'col'=16] {'row'}, use_global_device_ids=true, to_apply=%region_28.0 | all-reduce | flops 256 | bytes 2048 | tf_op jit(solution)/shard_map/psum | solution.py:50
  1078.4 0.9 multiply_reduce_fusion.10
  1079.3 30.2 %psum.181 = f32[256]{0:T(256)S(1)} all-reduce(f32[256]{0:T(256)S(1)} %get-tuple-element.19), channel_id=1, replica_groups=mesh['row'=8,'col'=16] {'col'}, use_global_device_ids=true, to_apply=%region_30.0 | all-reduce | flops 256 | bytes 2048 | tf_op jit(solution)/shard_map/psum | solution.py:50
  1109.6 19.6 %psum.182 = f32[256]{0:T(256)S(1)} all-reduce(f32[256]{0:T(256)S(1)} %psum.181), channel_id=1, replica_groups=mesh['row'=8,'col'=16] {'row'}, use_global_device_ids=true, to_apply=%region_31.0 | all-reduce | flops 256 | bytes 2048 | tf_op jit(solution)/shard_map/psum | solution.py:50
  1129.3 62.0 %psum.183 = f32[256]{0:T(256)S(1)} all-reduce(f32[256]{0:T(256)S(1)} %multiply_reduce_fusion.9), channel_id=1, replica_groups=mesh['row'=8,'col'=16] {'row','col'}, use_global_device_ids=true, to_apply=%region_33.0 | all-reduce | flops 256 | bytes 2048 | tf_op jit(solution)/shard_map/psum | solution.py:38
  1192.0 64.1 %all-gather.14.cloned.1.call-done = bf16[8192,256]{1,0:T(8,128)(2,1)} async-done(((bf16[64,256]{1,0:T(8,128)(2,1)}), bf16[8192,256]{1,0:T(8,128)(2,1)}) %all-gather.14.cloned.1.call-update) | async-done | bytes 4194320 | tf_op jit(solution)/shard_map/all_gather | solution.py:29
  1256.0 7.4 convolution_bitcast_fusion
  1263.4 6.5 copy.15
  1270.1 4.4 multiply_reduce_fusion
  1274.5 69.6 %reduce-scatter.14.cloned.1.call-done = f32[64,256]{1,0:T(8,128)} async-done(((f32[1024,256]{1,0:T(8,128)}), f32[64,256]{1,0:T(8,128)}) %reduce-scatter.14.cloned.1.call-update) | async-done | bytes 65552 | tf_op jit(solution)/shard_map/reduce_scatter | solution.py:35
  1344.1 0.9 multiply_reduce_fusion.8
  1344.9 30.9 %psum.184 = f32[256]{0:T(256)S(1)} all-reduce(f32[256]{0:T(256)S(1)} %multiply_reduce_fusion.8), channel_id=1, replica_groups=mesh['row'=8,'col'=16] {'col'}, use_global_device_ids=true, to_apply=%region_37.0 | all-reduce | flops 256 | bytes 2048 | tf_op jit(solution)/shard_map/psum | solution.py:50
  1375.8 21.4 %psum.185 = f32[256]{0:T(256)S(1)} all-reduce(f32[256]{0:T(256)S(1)} %psum.184), channel_id=1, replica_groups=mesh['row'=8,'col'=16] {'row'}, use_global_device_ids=true, to_apply=%region_38.0 | all-reduce | flops 256 | bytes 2048 | tf_op jit(solution)/shard_map/psum | solution.py:50
  1397.3 0.9 multiply_reduce_fusion.7
  1398.1 28.8 %psum.186 = f32[256]{0:T(256)S(1)} all-reduce(f32[256]{0:T(256)S(1)} %multiply_reduce_fusion.7), channel_id=1, replica_groups=mesh['row'=8,'col'=16] {'col'}, use_global_device_ids=true, to_apply=%region_40.0 | all-reduce | flops 256 | bytes 2048 | tf_op jit(solution)/shard_map/psum | solution.py:50
  1426.9 18.9 %psum.187 = f32[256]{0:T(256)S(1)} all-reduce(f32[256]{0:T(256)S(1)} %psum.186), channel_id=1, replica_groups=mesh['row'=8,'col'=16] {'row'}, use_global_device_ids=true, to_apply=%region_41.0 | all-reduce | flops 256 | bytes 2048 | tf_op jit(solution)/shard_map/psum | solution.py:50
  1445.9 0.9 multiply_reduce_fusion.6
  1446.8 30.2 %psum.188 = f32[256]{0:T(256)S(1)} all-reduce(f32[256]{0:T(256)S(1)} %get-tuple-element.17), channel_id=1, replica_groups=mesh['row'=8,'col'=16] {'col'}, use_global_device_ids=true, to_apply=%region_43.0 | all-reduce | flops 256 | bytes 2048 | tf_op jit(solution)/shard_map/psum | solution.py:50
  1477.0 19.6 %psum.189 = f32[256]{0:T(256)S(1)} all-reduce(f32[256]{0:T(256)S(1)} %psum.188), channel_id=1, replica_groups=mesh['row'=8,'col'=16] {'row'}, use_global_device_ids=true, to_apply=%region_44.0 | all-reduce | flops 256 | bytes 2048 | tf_op jit(solution)/shard_map/psum | solution.py:50
  1496.7 28.5 %psum.190 = f32[256]{0:T(256)S(1)} all-reduce(f32[256]{0:T(256)S(1)} %multiply_reduce_fusion.5), channel_id=1, replica_groups=mesh['row'=8,'col'=16] {'col'}, use_global_device_ids=true, to_apply=%region_46.0 | all-reduce | flops 256 | bytes 2048 | tf_op jit(solution)/shard_map/psum | solution.py:50
  1525.2 19.4 %psum.191 = f32[1,256]{1,0:T(1,128)S(1)} all-reduce(f32[1,256]{1,0:T(1,128)S(1)} %bitcast.76), channel_id=1, replica_groups=mesh['row'=8,'col'=16] {'row'}, use_global_device_ids=true, to_apply=%region_47.0 | all-reduce | flops 256 | bytes 2048 | tf_op jit(solution)/shard_map/psum | solution.py:50
  (79 shorter events, 3.9 us)
Async XLA Ops:
  6.5 1.6 copy-start
  6.5 74.1 %all-gather.6.cloned.1.call-start = ((), (), s32[]{:S(2)}) async-start(), calls=%async_computation.5 | async-start | bytes 4227072 | tf_op jit(solution)/shard_map/all_gather | solution.py:29
  8.0 160.5 %reduce-scatter.6.cloned.1.call-start = ((), (), s32[]{:S(2)}) async-start(), calls=%async_computation.6 | async-start | bytes 1114112 | tf_op jit(solution)/shard_map/reduce_scatter | solution.py:35
  98.9 201.5 %all-gather.8.cloned.1.call-start = ((), (), s32[]{:S(2)}) async-start(), calls=%async_computation.7 | async-start | bytes 4227072 | tf_op jit(solution)/shard_map/all_gather | solution.py:29
  237.0 151.4 %reduce-scatter.8.cloned.1.call-start = ((), (), s32[]{:S(2)}) async-start(), calls=%async_computation.8 | async-start | bytes 1114112 | tf_op jit(solution)/shard_map/reduce_scatter | solution.py:35
  314.4 74.0 %copy-start.2 = (f32[64,256]{1,0:T(8,128)S(1)}, f32[64,256]{1,0:T(8,128)}, u32[]{:S(2)}) copy-start(f32[64,256]{1,0:T(8,128)} %reduce-scatter.6.cloned.1.call-done) | copy-start | bytes 196612
  318.8 251.2 %all-gather.10.cloned.1.call-start = ((), (), s32[]{:S(2)}) async-start(), calls=%async_computation.9 | async-start | bytes 4227072 | tf_op jit(solution)/shard_map/all_gather | solution.py:29
  505.9 151.9 %reduce-scatter.10.cloned.1.call-start = ((), (), s32[]{:S(2)}) async-start(), calls=%async_computation.10 | async-start | bytes 1114112 | tf_op jit(solution)/shard_map/reduce_scatter | solution.py:35
  583.9 127.4 %copy-start.3 = (f32[64,256]{1,0:T(8,128)S(1)}, f32[64,256]{1,0:T(8,128)}, u32[]{:S(2)}) copy-start(f32[64,256]{1,0:T(8,128)} %reduce-scatter.8.cloned.1.call-done) | copy-start | bytes 196612
  588.3 300.4 %all-gather.12.cloned.1.call-start = ((), (), s32[]{:S(2)}) async-start(), calls=%async_computation.11 | async-start | bytes 4227072 | tf_op jit(solution)/shard_map/all_gather | solution.py:29
  824.7 151.9 %reduce-scatter.12.cloned.1.call-start = ((), (), s32[]{:S(2)}) async-start(), calls=%async_computation.12 | async-start | bytes 1114112 | tf_op jit(solution)/shard_map/reduce_scatter | solution.py:35
  907.0 349.0 %all-gather.14.cloned.1.call-start = ((), (), s32[]{:S(2)}) async-start(), calls=%async_computation.13 | async-start | bytes 4227072 | tf_op jit(solution)/shard_map/all_gather | solution.py:29
  1191.9 152.1 %reduce-scatter.14.cloned.1.call-start = ((), (), s32[]{:S(2)}) async-start(), calls=%async_computation.14 | async-start | bytes 1114112 | tf_op jit(solution)/shard_map/reduce_scatter | solution.py:35
  1263.4 282.4 %copy-start.1 = (f32[64,6]{0,1:T(8,128)S(1)}, f32[64,6]{0,1:T(8,128)}, u32[]{:S(2)}) copy-start(f32[64,6]{0,1:T(8,128)} %param.9) | copy-start | bytes 4612
  1270.0 274.8 %copy-start.12 = (f32[4,256]{1,0:T(4,128)S(1)}, f32[4,256]{1,0:T(4,128)}, u32[]{:S(2)}) copy-start(f32[4,256]{1,0:T(4,128)} %constant.71.clone.1) | copy-start | bytes 12292
  1270.0 274.8 %copy-start.11 = (f32[4,256]{1,0:T(4,128)S(1)}, f32[4,256]{1,0:T(4,128)}, u32[]{:S(2)}) copy-start(f32[4,256]{1,0:T(4,128)} %constant.72.clone.1) | copy-start | bytes 12292
  1270.0 274.8 %copy-start.10 = (f32[4,256]{1,0:T(4,128)S(1)}, f32[4,256]{1,0:T(4,128)}, u32[]{:S(2)}) copy-start(f32[4,256]{1,0:T(4,128)} %constant.73.clone.1) | copy-start | bytes 12292
  1270.0 274.9 %copy-start.9 = (f32[4,256]{1,0:T(4,128)S(1)}, f32[4,256]{1,0:T(4,128)}, u32[]{:S(2)}) copy-start(f32[4,256]{1,0:T(4,128)} %constant.74.clone.1) | copy-start | bytes 12292
  1270.0 274.9 %copy-start.8 = (f32[4,256]{1,0:T(4,128)S(1)}, f32[4,256]{1,0:T(4,128)}, u32[]{:S(2)}) copy-start(f32[4,256]{1,0:T(4,128)} %constant.75.clone.1) | copy-start | bytes 12292
  1270.0 275.0 %copy-start.7 = (f32[4,256]{1,0:T(4,128)S(1)}, f32[4,256]{1,0:T(4,128)}, u32[]{:S(2)}) copy-start(f32[4,256]{1,0:T(4,128)} %constant.76.clone.1) | copy-start | bytes 12292
  1270.0 275.0 %copy-start.6 = (f32[4,256]{1,0:T(4,128)S(1)}, f32[4,256]{1,0:T(4,128)}, u32[]{:S(2)}) copy-start(f32[4,256]{1,0:T(4,128)} %constant.77.clone.1) | copy-start | bytes 12292
  1270.0 275.0 %copy-start.5 = (f32[4,256]{1,0:T(4,128)S(1)}, f32[4,256]{1,0:T(4,128)}, u32[]{:S(2)}) copy-start(f32[4,256]{1,0:T(4,128)} %constant.78.clone.1) | copy-start | bytes 12292
  1270.0 275.1 %copy-start.4 = (f32[64,256]{1,0:T(8,128)S(1)}, f32[64,256]{1,0:T(8,128)}, u32[]{:S(2)}) copy-start(f32[64,256]{1,0:T(8,128)} %param.7) | copy-start | bytes 196612
Sparse Core Ops, SparseCore 0:
  10.5 70.1 all-gather.5
  99.1 69.4 reduce-scatter.5
  237.1 63.3 all-gather.7
  318.9 69.4 reduce-scatter.7
  506.0 63.9 all-gather.9
  588.4 69.3 reduce-scatter.9
  824.8 63.8 all-gather.11
  907.2 69.4 reduce-scatter.11
  1192.0 63.9 all-gather.13
  1274.6 69.4 reduce-scatter.13
